TPU v7x, 32 devices: a whole 2x2x4 slice. The times are simulated.
32 devices in a mesh: seq: 8 (over y, x, core), exp: 4 (over z).
Axes of the slice: x: 2, y: 2, z: 4, core: 2. Of those that a mesh axis runs over, the one named last changes fastest.
Arguments:
- queries: bfloat16 [4096, 2048], P('seq', 'exp'), may hold values from -6 to 6
- keys: bfloat16 [4096, 2048], P('seq', 'exp'), may hold values from -6 to 6
- values: bfloat16 [4096, 2048], P('seq', 'exp'), may hold values from -6 to 6
- head_gain: float32 [2048], P('exp'), may hold values from 0.5 to 1.5
- chosen: int32 [64, 3], replicated, may hold values from -1 to 55, as said below
- moe_input: bfloat16 [64, 7168], P('exp', 'seq'), may hold values from -6 to 6
- expert_ids: int32 [64, 2], P('exp'), may hold values from 0 to 3, all different within a row; in each aligned block of 16 rows (0 to 15, 16 to 31, ...) at most 12 rows name the same one
- route_weight: float32 [64, 2], P('exp'), may hold values from 0.05 to 0.5
- w_gate: bfloat16 [4, 7168, 2048], P('exp', 'seq'), may hold values from -0.09375 to 0.09375
- w_up: bfloat16 [4, 7168, 2048], P('exp', 'seq'), may hold values from -0.09375 to 0.09375
- w_down: bfloat16 [4, 2048, 7168], P('exp', None, 'seq'), may hold values from -0.125 to 0.125
Outputs:
- attention_out: bfloat16 [4096, 2048], P('seq', 'exp')
- moe_out: bfloat16 [64, 7168], P('exp', 'seq')
Inputs may be any that keep to these rules, and one draw needn't show every extreme that they name: `chosen`: each entry names a group of an earlier segment than the query block's own, or is -1. The groups in one row lie in different segments; -1 stands exactly where the block's segment has fewer than 3 earlier segments, and then all of them are named. Query blocks of one segment that name groups of the same earlier segment name the same group of it. `expert_ids`: among the 16 rows of one index of exp, no expert is named by more than 12 rows.
All inputs are finite; a program needn't handle non-finite values.
Results may differ from a plain program's by a relative error of at most 0.0057.
Values may be sent and summed in bfloat16 or wider, within the bound.
A program may use at most 64 MiB of HBM per device.

v0:
```python
import jax
import jax.numpy as jnp
from jax import lax
from jax.sharding import PartitionSpec as P

QK = 128
VD = 128
GROUP = 64
TOPK = 3


EPSILON = 1e-06
NEGATIVE = -1e30


def pool_groups(source):
    total = jnp.sum(source.reshape(-1, GROUP, source.shape[1]), axis=1, dtype=jnp.float32)
    return (total * GROUP ** (-0.5)).astype(jnp.bfloat16)


def head_attention(
    query_block_tiles,
    nearby_keys,
    nearby_values,
    compressed_keys,
    compressed_values,
    pool_mask,
    selected_keys,
    selected_values,
    picked_mask,
):
    block_count, block_width, depth = query_block_tiles.shape
    logit_scale = depth ** (-0.5)
    nearby_scores = (
        jnp.einsum(
            "rgo,uo->rgu", query_block_tiles, nearby_keys, preferred_element_type=jnp.float32
        )
        * logit_scale
    )
    query_pos = jnp.arange(block_count * block_width, dtype=jnp.int32).reshape(
        block_count, block_width
    )
    causal = (
        query_pos[:, :, None] >= jnp.arange(nearby_keys.shape[0], dtype=jnp.int32)[None, None, :]
    )
    nearby_scores = jnp.where(causal, nearby_scores, NEGATIVE)
    compressed_scores = (
        jnp.einsum(
            "nth,zh->ntz", query_block_tiles, compressed_keys, preferred_element_type=jnp.float32
        )
        * logit_scale
    )
    compressed_scores = jnp.where(pool_mask[None, None, :], compressed_scores, NEGATIVE)
    selected_scores = (
        jnp.einsum(
            "jae,jve->jav", query_block_tiles, selected_keys, preferred_element_type=jnp.float32
        )
        * logit_scale
    )
    selected_scores = jnp.where(picked_mask[:, None, :], selected_scores, NEGATIVE)
    highest = jnp.maximum(
        jnp.maximum(jnp.max(nearby_scores, axis=-1), jnp.max(compressed_scores, axis=-1)),
        jnp.max(selected_scores, axis=-1),
    )[:, :, None]
    nearby_probabilities = jnp.exp(nearby_scores - highest)
    compressed_probabilities = jnp.exp(compressed_scores - highest)
    selected_probabilities = jnp.exp(selected_scores - highest)
    denominator = (
        jnp.sum(nearby_probabilities, axis=-1)
        + jnp.sum(compressed_probabilities, axis=-1)
        + jnp.sum(selected_probabilities, axis=-1)
    )
    blended_output = jnp.einsum(
        "epc,cf->epf",
        nearby_probabilities.astype(jnp.bfloat16),
        nearby_values,
        preferred_element_type=jnp.float32,
    )
    blended_output = blended_output + jnp.einsum(
        "trx,xv->trv",
        compressed_probabilities.astype(jnp.bfloat16),
        compressed_values,
        preferred_element_type=jnp.float32,
    )
    blended_output = blended_output + jnp.einsum(
        "gvc,gcr->gvr",
        selected_probabilities.astype(jnp.bfloat16),
        selected_values,
        preferred_element_type=jnp.float32,
    )
    return blended_output / denominator[:, :, None]


def head_norm(blended_output, gain):
    mean_square = jnp.mean(blended_output * blended_output, axis=-1, keepdims=True)
    return (blended_output * lax.rsqrt(mean_square + EPSILON) * gain).astype(jnp.bfloat16)


def attention_part(queries, keys, values, head_gain, chosen):
    seg_count = lax.axis_size("seq")
    device = lax.axis_index("seq")
    length = queries.shape[0]
    head_count = queries.shape[1] // QK
    block_count = length // GROUP
    compressed_keys, compressed_values = (
        lax.all_gather(pool_groups(keys), "seq", axis=0, tiled=True),
        lax.all_gather(pool_groups(values), "seq", axis=0, tiled=True),
    )
    by_device = chosen.reshape(seg_count, block_count * TOPK)
    wanted = jnp.max(
        jnp.where(by_device // block_count == device, by_device % block_count, -1), axis=1
    )
    picker = (wanted[:, None] == jnp.arange(block_count, dtype=jnp.int32)[None, :]).astype(
        jnp.bfloat16
    )
    key_rows = jnp.dot(
        picker, keys.reshape(block_count, -1), preferred_element_type=jnp.float32
    ).astype(jnp.bfloat16)
    value_rows = jnp.dot(
        picker, values.reshape(block_count, -1), preferred_element_type=jnp.float32
    ).astype(jnp.bfloat16)
    arrived_keys, arrived_values = (
        lax.all_to_all(key_rows, "seq", split_axis=0, concat_axis=0, tiled=True),
        lax.all_to_all(value_rows, "seq", split_axis=0, concat_axis=0, tiled=True),
    )
    own_rows = lax.dynamic_slice_in_dim(chosen, device * block_count, block_count, 0)
    source_index = jnp.maximum(own_rows, 0) // block_count
    selected_keys = arrived_keys[source_index].reshape(block_count, TOPK * GROUP, -1)
    selected_values = arrived_values[source_index].reshape(block_count, TOPK * GROUP, -1)
    picked_mask = jnp.repeat(own_rows >= 0, GROUP, axis=1)
    pool_mask = jnp.arange(seg_count * block_count, dtype=jnp.int32) < device * block_count
    query_block_tiles = queries.reshape(block_count, GROUP, -1)
    results = []
    for head_index in range(head_count):
        qk_cols = slice(head_index * QK, (head_index + 1) * QK)
        vd_cols = slice(head_index * VD, (head_index + 1) * VD)
        blended_output = head_attention(
            query_block_tiles[:, :, qk_cols],
            keys[:, qk_cols],
            values[:, vd_cols],
            compressed_keys[:, qk_cols],
            compressed_values[:, vd_cols],
            pool_mask,
            selected_keys[:, :, qk_cols],
            selected_values[:, :, vd_cols],
            picked_mask,
        )
        results.append(head_norm(blended_output, head_gain[vd_cols]))
    return jnp.concatenate(results, axis=-1).reshape(length, -1)


def expert_part(moe_input, expert_ids, route_weight, w_gate, w_up, w_down):
    tok_rows, slab_width = moe_input.shape
    expert_count = lax.axis_size("exp")
    top_count = expert_ids.shape[1]
    capacity = 3 * tok_rows // 4
    assignments = tok_rows * top_count
    flat_ids = expert_ids.reshape(assignments)
    onehot = (flat_ids[:, None] == jnp.arange(expert_count, dtype=jnp.int32)[None, :]).astype(
        jnp.float32
    )
    earlier_mask = (
        jnp.arange(assignments, dtype=jnp.int32)[:, None]
        > jnp.arange(assignments, dtype=jnp.int32)[None, :]
    ).astype(jnp.float32)
    before = jnp.dot(earlier_mask, onehot, precision=lax.Precision.HIGHEST)
    slot_index = jnp.sum(before * onehot, axis=1).astype(jnp.int32)
    target = flat_ids * capacity + slot_index
    placement = (
        jnp.arange(expert_count * capacity, dtype=jnp.int32)[:, None] == target[None, :]
    ).astype(jnp.float32)
    placement = placement.reshape(expert_count * capacity, tok_rows, top_count)
    route_rows = jnp.sum(placement, axis=2).astype(jnp.bfloat16)
    weighting = jnp.sum(placement * route_weight[None, :, :], axis=2)
    outgoing = jnp.dot(route_rows, moe_input, preferred_element_type=jnp.float32).astype(
        jnp.bfloat16
    )
    outgoing = outgoing.reshape(expert_count, capacity, slab_width)
    gate_local = w_gate[0]
    up_local = w_up[0]
    down_local = w_down[0]
    arrived = lax.all_to_all(outgoing, "exp", split_axis=0, concat_axis=0, tiled=True)
    sources, items, width = arrived.shape
    row_block = arrived.reshape(sources * items, width)
    gate_part = jnp.dot(row_block, gate_local, preferred_element_type=jnp.float32)
    up_part = jnp.dot(row_block, up_local, preferred_element_type=jnp.float32)
    gate_total, up_total = lax.psum((gate_part, up_part), "seq")
    hidden = (jax.nn.silu(gate_total) * up_total).astype(jnp.bfloat16)
    produced = jnp.dot(hidden, down_local, preferred_element_type=jnp.float32).astype(jnp.bfloat16)
    processed = produced.reshape(sources, items, -1)
    returned = lax.all_to_all(processed, "exp", split_axis=0, concat_axis=0, tiled=True)
    returned = returned.reshape(expert_count * capacity, slab_width).astype(jnp.float32)
    combined = jnp.dot(weighting.T, returned, precision=lax.Precision.HIGHEST)
    return combined.astype(jnp.bfloat16)


def local(
    queries,
    keys,
    values,
    head_gain,
    chosen,
    moe_input,
    expert_ids,
    route_weight,
    w_gate,
    w_up,
    w_down,
):
    attention_out = attention_part(queries, keys, values, head_gain, chosen)
    moe_out = expert_part(moe_input, expert_ids, route_weight, w_gate, w_up, w_down)
    return (attention_out, moe_out)


def solution(mesh):
    placed = (
        P("seq", "exp"),
        P("seq", "exp"),
        P("seq", "exp"),
        P("exp"),
        P(),
        P("exp", "seq"),
        P("exp", None),
        P("exp", None),
        P("exp", "seq", None),
        P("exp", "seq", None),
        P("exp", None, "seq"),
    )
    return jax.shard_map(
        local,
        mesh=mesh,
        in_specs=placed,
        out_specs=(P("seq", "exp"), P("exp", "seq")),
        check_vma=False,
    )
```

profile of v0, /device:TPU:0, one launch (start us, length us, event | category | flops | bytes accessed | tf_op | source)
XLA Modules:
  0.0 155.2 jit_solution(15644187737860074799)
XLA Ops:
  9.2 1.4 convert_reduce_fusion.2
  11.4 6.3 %all-to-all-start.2 = ((bf16[4,12,896]{2,1,0:T(8,128)(2,1)}), bf16[4,12,896]{2,1,0:T(8,128)(2,1)S(1)}, u32[]{:S(2)}, u32[]{:S(2)}) async-start(bf16[4,12,896]{2,1,0:T(8,128)(2,1)} %reshape.190), calls=%async_computation.2 | async-start | bytes 229376 | tf_op jit(solution)/shard_map/all_to_all | solution.py:182
  17.7 1.3 reshape.185
  20.2 9.3 %all_gather.6 = bf16[64,512]{1,0:T(8,128)(2,1)S(1)} all-gather(bf16[8,512]{1,0:T(8,128)(2,1)S(1)} %multiply_convert_fusion.7), channel_id=1, replica_groups=mesh['seq'=8,'exp'=4] {'seq'}, dimensions={0}, use_global_device_ids=true | all-gather | bytes 73728 | tf_op jit(solution)/shard_map/all_gather | solution.py:106
  29.5 1.6 %fusion.147 = (f32[8,64]{1,0:T(8,128)}, f32[8,64,64]{1,2,0:T(8,128)}) fusion(bf16[8,64,512]{2,1,0:T(8,128)(2,1)S(1)} %bitcast.120, bf16[64,512]{1,0:T(8,128)(2,1)S(1)} %all_gather.6, pred[64]{0:T(512)(128)(4,1)S(1)} %iota_compare_fusion.9), kind=kOutput, calls=%fused_computation.230 | convolution fusion | flops 8486400 | bytes 281088 | tf_op jit(solution)/shard_map/nth,zh->ntz/dot_general | solution.py:48
  31.9 1.9 %fusion.146 = (f32[8,64]{1,0:T(8,128)}, f32[8,64,512]{2,1,0:T(8,128)}) fusion(bf16[512,512]{1,0:T(8,128)(2,1)S(1)} %copy-done.8, bf16[8,64,512]{2,1,0:T(8,128)(2,1)S(1)} %bitcast.122, s32[8,64]{1,0:T(8,128)S(1)} %multiply_add_fusion), kind=kOutput, calls=%fused_computation.229 | convolution fusion | flops 68156928 | bytes 1316864 | tf_op jit(solution)/shard_map/rgo,uo->rgu/dot_general | solution.py:35
  33.8 1.9 %fusion.143 = (f32[8,64]{1,0:T(8,128)}, f32[8,64,512]{2,1,0:T(8,128)}) fusion(bf16[512,512]{1,0:T(8,128)(2,1)S(1)} %copy-done.8, bf16[8,64,512]{2,1,0:T(8,128)(2,1)S(1)} %bitcast.123, s32[8,64]{1,0:T(8,128)S(1)} %multiply_add_fusion), kind=kOutput, calls=%fused_computation.226 | convolution fusion | flops 68156928 | bytes 1316864 | tf_op jit(solution)/shard_map/rgo,uo->rgu/dot_general | solution.py:35
  36.5 1.9 %fusion.140 = (f32[8,64]{1,0:T(8,128)}, f32[8,64,512]{2,1,0:T(8,128)}) fusion(bf16[512,512]{1,0:T(8,128)(2,1)S(1)} %copy-done.8, bf16[8,64,512]{2,1,0:T(8,128)(2,1)S(1)} %bitcast.125, s32[8,64]{1,0:T(8,128)S(1)} %multiply_add_fusion), kind=kOutput, calls=%fused_computation.223 | convolution fusion | flops 68156928 | bytes 1316864 | tf_op jit(solution)/shard_map/rgo,uo->rgu/dot_general | solution.py:35
  39.2 2.5 %fusion.137 = (f32[8,64]{1,0:T(8,128)}, f32[8,64,512]{2,1,0:T(8,128)}) fusion(bf16[512,512]{1,0:T(8,128)(2,1)S(1)} %copy-done.8, bf16[8,64,512]{2,1,0:T(8,128)(2,1)S(1)} %bitcast.127, s32[8,64]{1,0:T(8,128)} %copy-done.29), kind=kOutput, calls=%fused_computation.220 | convolution fusion | flops 68156928 | bytes 1314816 | tf_op jit(solution)/shard_map/rgo,uo->rgu/dot_general | solution.py:35
  42.6 1.3 multiply_convert_fusion.6
  45.9 1.4 fusion.135
  52.7 1.2 reshape.236
  53.9 10.2 %all_gather.7 = bf16[64,512]{1,0:T(8,128)(2,1)} all-gather(bf16[8,512]{1,0:T(8,128)(2,1)S(1)} %copy-done.21), channel_id=1, replica_groups=mesh['seq'=8,'exp'=4] {'seq'}, dimensions={0}, use_global_device_ids=true | all-gather | bytes 73728 | tf_op jit(solution)/shard_map/all_gather | solution.py:107
  64.0 3.5 %all-to-all-start = ((bf16[8,2,16384]{2,1,0:T(2,128)(2,1)}), bf16[8,2,16384]{2,1,0:T(2,128)(2,1)S(1)}, u32[]{:S(2)}, u32[]{:S(2)}) async-start(bf16[8,2,16384]{2,1,0:T(2,128)(2,1)} %reshape.234), calls=%async_computation | async-start | bytes 1048576 | tf_op jit(solution)/shard_map/all_to_all | solution.py:123
  67.7 3.8 %fusion.4 = f32[48,2048]{1,0:T(8,128)} fusion(bf16[48,896]{1,0:T(8,128)(2,1)S(1)} %reshape.191, bf16[1,896,2048]{2,1,0:T(8,128)(2,1)} %param.20), kind=kOutput, calls=%fused_computation.8 | convolution fusion | flops 176160768 | bytes 4149248 | tf_op jit(solution)/shard_map/dot_general | solution.py:186
  71.4 1.5 fusion.6
  73.0 4.2 %all-to-all-done = bf16[8,2,16384]{2,1,0:T(2,128)(2,1)S(1)} async-done(((bf16[8,2,16384]{2,1,0:T(2,128)(2,1)}), bf16[8,2,16384]{2,1,0:T(2,128)(2,1)S(1)}, u32[]{:S(2)}, u32[]{:S(2)}) %all-to-all-start) | async-done | bytes 524320 | tf_op jit(solution)/shard_map/all_to_all | solution.py:123
  77.2 4.3 %all-to-all-start.1 = ((bf16[8,2,16384]{2,1,0:T(2,128)(2,1)}), bf16[8,2,16384]{2,1,0:T(2,128)(2,1)}, u32[]{:S(2)}, u32[]{:S(2)}) async-start(bf16[8,2,16384]{2,1,0:T(2,128)(2,1)} %reshape.236), calls=%async_computation.1 | async-start | bytes 1048576 | tf_op jit(solution)/shard_map/all_to_all | solution.py:124
  82.7 1.6 %gather_fusion = bf16[24,32768]{1,0:T(8,128)(2,1)S(1)} fusion(bf16[8,32768]{1,0:T(8,128)(2,1)S(1)} %bitcast.118, s32[1024]{0:T(1024)S(1)} %pad_clamp_fusion), kind=kCustom, calls=%fused_computation | custom fusion | bytes 3145824 | tf_op jit(solution)/shard_map/gather | solution.py:128
  84.3 2.1 %reshape.186 = bf16[8,192,512]{2,1,0:T(8,128)(2,1)} reshape(bf16[24,32768]{1,0:T(8,128)(2,1)S(1)} %gather_fusion) | data formatting | bytes 3145728 | tf_op jit(solution)/shard_map/reshape | solution.py:128
  86.4 1.6 %fusion.145 = (f32[8,64]{1,0:T(8,128)S(1)}, f32[8,64,192]{2,1,0:T(8,128)S(1)}) fusion(bf16[8,64,512]{2,1,0:T(8,128)(2,1)S(1)} %bitcast.128, bf16[8,192,512]{2,1,0:T(8,128)(2,1)} %reshape.186, pred[8,192]{1,0:T(8,128)(4,1)S(1)} %copy-done.38), kind=kOutput, calls=%fused_computation.228 | convolution fusion | flops 25460224 | bytes 921600 | tf_op jit(solution)/shard_map/jae,jve->jav/dot_general | solution.py:55
  89.6 1.2 fusion.142
  92.3 1.2 fusion.139
  94.9 2.1 %fusion.136 = (f32[8,64]{1,0:T(8,128)S(1)}, f32[8,64,192]{2,1,0:T(8,128)}) fusion(bf16[8,64,512]{2,1,0:T(8,128)(2,1)} %bitcast.119, bf16[8,192,512]{2,1,0:T(8,128)(2,1)S(1)} %copy-done.10, pred[8,192]{1,0:T(8,128)(4,1)S(1)} %copy-done.38), kind=kOutput, calls=%fused_computation.219 | convolution fusion | flops 25460224 | bytes 921600 | tf_op jit(solution)/shard_map/jae,jve->jav/dot_general | solution.py:55
  98.2 2.2 %reshape.237 = bf16[8,1,32768]{2,1,0:T(2,128)(2,1)S(1)} reshape(bf16[8,2,16384]{2,1,0:T(2,128)(2,1)} %all-to-all-done.1) | data formatting | bytes 1048576
  101.0 1.6 %gather_fusion.1 = bf16[24,32768]{1,0:T(8,128)(2,1)S(1)} fusion(bf16[8,32768]{1,0:T(8,128)(2,1)S(1)} %bitcast.117, s32[1024]{0:T(1024)S(1)} %pad_clamp_fusion), kind=kCustom, calls=%fused_computation.1 | custom fusion | bytes 3145824 | tf_op jit(solution)/shard_map/gather | solution.py:129
  102.6 2.1 %reshape.188 = bf16[8,192,512]{2,1,0:T(8,128)(2,1)} reshape(bf16[24,32768]{1,0:T(8,128)(2,1)S(1)} %gather_fusion.1) | data formatting | bytes 3145728 | tf_op jit(solution)/shard_map/reshape | solution.py:129
  105.0 1.7 %multiply_reduce_fusion.3 = (f32[8,64]{1,0:T(8,128)S(1)}, f32[8,64,128]{2,1,0:T(8,128)S(1)}) fusion(f32[8,64]{1,0:T(8,128)S(1)} %add_add_fusion.3, f32[8,64,128]{2,1,0:T(8,128)S(1)} %convolution_add_fusion.7, bf16[8,192,512]{2,1,0:T(8,128)(2,1)} %reshape.188, f32[8,64,192]{2,1,0:T(8,128)} %copy-done.19, f32[8,64]{1,0:T(8,128)S(1)} %maximum_maximum_fusion.3), kind=kOutput, calls=%fused_computation.121 | convolution fusion | flops 25624064 | bytes 1447936 | tf_op jit(solution)/shard_map/gvc,gcr->gvr/dot_general | solution.py:85
  110.6 22.8 %all-reduce.3.cloned.1.call-done = (f32[48,2048]{1,0:T(8,128)}, f32[48,2048]{1,0:T(8,128)}) async-done(((f32[48,2048]{1,0:T(8,128)}, f32[48,2048]{1,0:T(8,128)}), (f32[48,2048]{1,0:T(8,128)}, f32[48,2048]{1,0:T(8,128)})) %all-reduce.3.cloned.1.call-update) | async-done | bytes 786448 | tf_op jit(solution)/shard_map/psum | solution.py:187
  133.5 3.0 %fusion.32 = bf16[48,896]{1,0:T(8,128)(2,1)S(1)} fusion(bf16[1,2048,896]{2,1,0:T(8,128)(2,1)} %param.21, f32[48,2048]{1,0:T(8,128)} %get-tuple-element.4, f32[48,2048]{1,0:T(8,128)} %get-tuple-element.5), kind=kOutput, calls=%fused_computation.56 | convolution fusion | flops 176793600 | bytes 4542464 | tf_op jit(solution)/shard_map/dot_general | solution.py:189
  137.1 4.5 %all-to-all-start.3 = ((bf16[4,12,896]{2,1,0:T(8,128)(2,1)}), bf16[4,12,896]{2,1,0:T(8,128)(2,1)S(1)}, u32[]{:S(2)}, u32[]{:S(2)}) async-start(bf16[4,12,896]{2,1,0:T(8,128)(2,1)} %reshape.192), calls=%async_computation.3 | async-start | bytes 229376 | tf_op jit(solution)/shard_map/all_to_all | solution.py:191
  142.7 4.8 %all-to-all-done.3 = bf16[4,12,896]{2,1,0:T(8,128)(2,1)S(1)} async-done(((bf16[4,12,896]{2,1,0:T(8,128)(2,1)}), bf16[4,12,896]{2,1,0:T(8,128)(2,1)S(1)}, u32[]{:S(2)}, u32[]{:S(2)}) %all-to-all-start.3) | async-done | bytes 86048 | tf_op jit(solution)/shard_map/all_to_all | solution.py:191
  (162 shorter events, 28.3 us)
Async XLA Ops:
  7.2 3.3 %copy-start = (bf16[16,896]{1,0:T(8,128)(2,1)S(1)}, bf16[16,896]{1,0:T(8,128)(2,1)}, u32[]{:S(2)}) copy-start(bf16[16,896]{1,0:T(8,128)(2,1)} %param.16) | copy-start | bytes 86020
  7.2 11.9 %copy-start.8 = (bf16[512,512]{1,0:T(8,128)(2,1)S(1)}, bf16[512,512]{1,0:T(8,128)(2,1)}, u32[]{:S(2)}) copy-start(bf16[512,512]{1,0:T(8,128)(2,1)} %param.12) | copy-start | bytes 1572868
  7.2 12.0 %copy-start.1 = (bf16[512,512]{1,0:T(8,128)(2,1)S(1)}, bf16[512,512]{1,0:T(8,128)(2,1)}, u32[]{:S(2)}) copy-start(bf16[512,512]{1,0:T(8,128)(2,1)} %param.13) | copy-start | bytes 1572868
  11.4 52.7 %all-to-all-start.2 = ((bf16[4,12,896]{2,1,0:T(8,128)(2,1)}), bf16[4,12,896]{2,1,0:T(8,128)(2,1)S(1)}, u32[]{:S(2)}, u32[]{:S(2)}) async-start(bf16[4,12,896]{2,1,0:T(8,128)(2,1)} %reshape.190), calls=%async_computation.2 | async-start | bytes 229376 | tf_op jit(solution)/shard_map/all_to_all | solution.py:182
  17.7 11.7 %copy-start.14 = (bf16[512,512]{1,0:T(8,128)(2,1)S(1)}, bf16[512,512]{1,0:T(8,128)(2,1)}, u32[]{:S(2)}) copy-start(bf16[512,512]{1,0:T(8,128)(2,1)} %param.11) | copy-start | bytes 1572868
  19.2 17.3 %copy-start.29 = (s32[8,64]{1,0:T(8,128)}, s32[8,64]{1,0:T(8,128)S(1)}, u32[]{:S(2)}) copy-start(s32[8,64]{1,0:T(8,128)S(1)} %multiply_add_fusion) | copy-start | bytes 6148
  36.5 5.3 %copy-start.23 = (s32[64,3]{0,1:T(4,128)S(1)}, s32[64,3]{0,1:T(4,128)}, u32[]{:S(2)}) copy-start(s32[64,3]{0,1:T(4,128)} %param.15) | copy-start | bytes 2308
  49.7 4.2 %copy-start.21 = (bf16[8,512]{1,0:T(8,128)(2,1)S(1)}, bf16[8,512]{1,0:T(8,128)(2,1)}, u32[]{:S(2)}) copy-start(bf16[8,512]{1,0:T(8,128)(2,1)} %multiply_convert_fusion.6) | copy-start | bytes 24580
  64.0 13.2 %all-to-all-start = ((bf16[8,2,16384]{2,1,0:T(2,128)(2,1)}), bf16[8,2,16384]{2,1,0:T(2,128)(2,1)S(1)}, u32[]{:S(2)}, u32[]{:S(2)}) async-start(bf16[8,2,16384]{2,1,0:T(2,128)(2,1)} %reshape.234), calls=%async_computation | async-start | bytes 1048576 | tf_op jit(solution)/shard_map/all_to_all | solution.py:123
  67.6 65.9 %all-reduce.3.cloned.1.call-start = ((), (), s32[]{:S(2)}) async-start(), calls=%async_computation.4 | async-start | bytes 1572864 | tf_op jit(solution)/shard_map/psum | solution.py:187
  67.6 3.8 %copy-start.6 = (bf16[1,896,2048]{2,1,0:T(8,128)(2,1)S(1)}, bf16[1,896,2048]{2,1,0:T(8,128)(2,1)}, u32[]{:S(2)}) copy-start(bf16[1,896,2048]{2,1,0:T(8,128)(2,1)} %param.19) | copy-start | bytes 11010052
  77.2 21.0 %all-to-all-start.1 = ((bf16[8,2,16384]{2,1,0:T(2,128)(2,1)}), bf16[8,2,16384]{2,1,0:T(2,128)(2,1)}, u32[]{:S(2)}, u32[]{:S(2)}) async-start(bf16[8,2,16384]{2,1,0:T(2,128)(2,1)} %reshape.236), calls=%async_computation.1 | async-start | bytes 1048576 | tf_op jit(solution)/shard_map/all_to_all | solution.py:124
  84.3 2.2 %copy-start.15 = (bf16[512,512]{1,0:T(8,128)(2,1)S(1)}, bf16[512,512]{1,0:T(8,128)(2,1)}, u32[]{:S(2)}) copy-start(bf16[512,512]{1,0:T(8,128)(2,1)} %param.11) | copy-start | bytes 1572868
  84.3 3.8 %copy-start.27 = (f32[8,64]{1,0:T(8,128)S(1)}, f32[8,64]{1,0:T(8,128)}, u32[]{:S(2)}) copy-start(f32[8,64]{1,0:T(8,128)} %get-tuple-element.38) | copy-start | bytes 6148
  84.3 3.8 %copy-start.33 = (f32[8,64]{1,0:T(8,128)S(1)}, f32[8,64]{1,0:T(8,128)}, u32[]{:S(2)}) copy-start(f32[8,64]{1,0:T(8,128)} %get-tuple-element.36) | copy-start | bytes 6148
  86.4 3.2 %copy-start.10 = (bf16[8,192,512]{2,1,0:T(8,128)(2,1)S(1)}, bf16[8,192,512]{2,1,0:T(8,128)(2,1)}, u32[]{:S(2)}) copy-start(bf16[8,192,512]{2,1,0:T(8,128)(2,1)} %reshape.186) | copy-start | bytes 4718596
  88.0 9.0 %copy-start.19 = (f32[8,64,192]{2,1,0:T(8,128)}, f32[8,64,192]{2,1,0:T(8,128)S(1)}, u32[]{:S(2)}) copy-start(f32[8,64,192]{2,1,0:T(8,128)S(1)} %get-tuple-element.35) | copy-start | bytes 1179652
  88.5 2.3 %copy-start.26 = (f32[8,64]{1,0:T(8,128)S(1)}, f32[8,64]{1,0:T(8,128)}, u32[]{:S(2)}) copy-start(f32[8,64]{1,0:T(8,128)} %get-tuple-element.30) | copy-start | bytes 6148
  88.5 2.3 %copy-start.32 = (f32[8,64]{1,0:T(8,128)S(1)}, f32[8,64]{1,0:T(8,128)}, u32[]{:S(2)}) copy-start(f32[8,64]{1,0:T(8,128)} %get-tuple-element.28) | copy-start | bytes 6148
  88.5 2.3 %copy-start.4 = (f32[8,64,512]{2,1,0:T(8,128)S(1)}, f32[8,64,512]{2,1,0:T(8,128)}, u32[]{:S(2)}) copy-start(f32[8,64,512]{2,1,0:T(8,128)} %get-tuple-element.29) | copy-start | bytes 3145732
  91.2 2.3 %copy-start.25 = (f32[8,64]{1,0:T(8,128)S(1)}, f32[8,64]{1,0:T(8,128)}, u32[]{:S(2)}) copy-start(f32[8,64]{1,0:T(8,128)} %get-tuple-element.22) | copy-start | bytes 6148
  91.2 2.3 %copy-start.31 = (f32[8,64]{1,0:T(8,128)S(1)}, f32[8,64]{1,0:T(8,128)}, u32[]{:S(2)}) copy-start(f32[8,64]{1,0:T(8,128)} %get-tuple-element.20) | copy-start | bytes 6148
  91.2 2.3 %copy-start.3 = (f32[8,64,512]{2,1,0:T(8,128)S(1)}, f32[8,64,512]{2,1,0:T(8,128)}, u32[]{:S(2)}) copy-start(f32[8,64,512]{2,1,0:T(8,128)} %get-tuple-element.21) | copy-start | bytes 3145732
  94.5 2.8 %copy-start.24 = (f32[8,64]{1,0:T(8,128)S(1)}, f32[8,64]{1,0:T(8,128)}, u32[]{:S(2)}) copy-start(f32[8,64]{1,0:T(8,128)} %get-tuple-element.14) | copy-start | bytes 6148
  94.5 2.8 %copy-start.30 = (f32[8,64]{1,0:T(8,128)S(1)}, f32[8,64]{1,0:T(8,128)}, u32[]{:S(2)}) copy-start(f32[8,64]{1,0:T(8,128)} %get-tuple-element.12) | copy-start | bytes 6148
  94.5 2.8 %copy-start.7 = (f32[8,64,64]{1,2,0:T(8,128)S(1)}, f32[8,64,64]{1,2,0:T(8,128)}, u32[]{:S(2)}) copy-start(f32[8,64,64]{1,2,0:T(8,128)} %get-tuple-element.39) | copy-start | bytes 393220
  94.5 2.9 %copy-start.2 = (f32[8,64,512]{2,1,0:T(8,128)S(1)}, f32[8,64,512]{2,1,0:T(8,128)}, u32[]{:S(2)}) copy-start(f32[8,64,512]{2,1,0:T(8,128)} %get-tuple-element.13) | copy-start | bytes 3145732
  105.0 2.3 %copy-start.9 = (bf16[8,192,512]{2,1,0:T(8,128)(2,1)S(1)}, bf16[8,192,512]{2,1,0:T(8,128)(2,1)}, u32[]{:S(2)}) copy-start(bf16[8,192,512]{2,1,0:T(8,128)(2,1)} %reshape.188) | copy-start | bytes 4718596
  133.4 8.2 %copy-start.34 = (f32[128]{0:T(128)S(1)}, f32[128]{0:T(128)}, u32[]{:S(2)}) copy-start(f32[128]{0:T(128)} %get-tuple-element.8) | copy-start | bytes 1540
  133.5 8.2 %copy-start.35 = (f32[128]{0:T(128)S(1)}, f32[128]{0:T(128)}, u32[]{:S(2)}) copy-start(f32[128]{0:T(128)} %get-tuple-element.9) | copy-start | bytes 1540
  136.4 11.1 %copy-start.22 = (f32[48,16]{0,1:T(8,128)S(1)}, f32[48,16]{0,1:T(8,128)}, u32[]{:S(2)}) copy-start(f32[48,16]{0,1:T(8,128)} %get-tuple-element.3) | copy-start | bytes 9220
  137.1 10.4 %all-to-all-start.3 = ((bf16[4,12,896]{2,1,0:T(8,128)(2,1)}), bf16[4,12,896]{2,1,0:T(8,128)(2,1)S(1)}, u32[]{:S(2)}, u32[]{:S(2)}) async-start(bf16[4,12,896]{2,1,0:T(8,128)(2,1)} %reshape.192), calls=%async_computation.3 | async-start | bytes 229376 | tf_op jit(solution)/shard_map/all_to_all | solution.py:191
  (12 other events, 18.2 us)
Sparse Core Ops, SparseCore 0:
  73.1 60.3 all-reduce.2
where the time goes:
time: 156 us; the launch traced here: 155 us
  matrix products  36.5 us (23%)
  waiting for transfers between devices  31.9 us (20%)
  local copies, waits for them, and re-layouts  22.7 us (15%)
  blocking collectives  19.4 us (12%)
  starting transfers between devices  18.8 us (12%)
  between operations  14.8 us (9%)
  other arithmetic  11.1 us (7%)
    psum x1, waiting for transfers between devices, expert_part(): gate_total, up_total = lax.psum((gate_part, up_part), 'seq')  22.8 us
    all_gather x1, blocking collectives, attention_part(): lax.all_gather(pool_groups(values), 'seq', axis=0, tiled=True)  10.2 us
    all_gather x1, blocking collectives, attention_part(): lax.all_gather(pool_groups(keys), 'seq', axis=0, tiled=True)  9.26 us
    unnamed x85, local copies, waits for them, and re-layouts  8.44 us
    dot_general x4, matrix products, head_attention(): jnp.einsum('rgo,uo->rgu', query_block_tiles, nearby_keys, preferred_eleme...  8.2 us
    all_to_all x1, starting transfers between devices, expert_part(): lax.all_to_all(outgoing, 'exp', split_axis=0, concat_axis=0, tiled=True)  6.34 us
    dot_general x4, matrix products, head_attention(): jnp.einsum('jae,jve->jav', query_block_tiles, selected_keys, preferred_el...  6.11 us
    all_to_all x1, waiting for transfers between devices, expert_part(): lax.all_to_all(processed, 'exp', split_axis=0, concat_axis=0, tiled=True)  4.79 us
  transfers between devices with their start and end apart: 5, of which 3 were waited for; matrix products, arithmetic and copies ran while one was open for 39% of the time, Pallas kernels for 0%

commit v1 on v0

v1 whole, which is shorter than its diff:
```python
import functools

import jax
import jax.numpy as jnp
from jax import lax
from jax.experimental import pallas as pl
from jax.experimental.pallas import tpu as pltpu
from jax.sharding import PartitionSpec as P

HEAD = 128
GROUP = 64
TOPK = 3
TILE = 128
EPSILON = 1e-06
NEGATIVE = -1e30
MESH = pl.DeviceIdType.MESH
F32 = jnp.float32
BF16 = jnp.bfloat16


def across(a, b):
    return lax.dot_general(a, b, (((1,), (1,)), ((), ())), preferred_element_type=F32)


def kernel(
    S, E,
    q_ref, k_ref, v_ref, gain_ref, chosen_ref, x_ref, ids_ref, rw_ref, wg_hbm, wu_hbm, wd_hbm,
    attn_ref, moe_ref,
    wg, wu, wd, kv_send, kv_all, pool_send, pool_all, pool_k, pool_v,
    acc, top, den, x_all, part, rs_all, hid_send, hid_all, ret_send, ret_all,
    w_sem, kv_ss, kv_rs, pool_ss, pool_rs, x_ss, x_rs, rs_ss, rs_rs, hid_ss, hid_rs, ret_ss, ret_rs,
):
    me = lax.axis_index("seq")
    ex = lax.axis_index("exp")
    L, C = q_ref.shape
    heads = C // HEAD
    nb = L // GROUP
    T, Dl = x_ref.shape
    FF = wg.shape[1]
    rows = E * T
    own = rows // S
    scale = HEAD ** (-0.5)

    weight_copies = [
        pltpu.make_async_copy(src, dst, w_sem.at[i])
        for i, (src, dst) in enumerate(((wg_hbm, wg), (wu_hbm, wu), (wd_hbm, wd)))
    ]
    for copy in weight_copies:
        copy.start()

    def seq_copy(src, dst, ss, rs, peer):
        return pltpu.make_async_remote_copy(
            src_ref=src, dst_ref=dst, send_sem=ss, recv_sem=rs,
            device_id={"seq": peer}, device_id_type=MESH,
        )

    def exp_copy(src, dst, ss, rs, peer):
        return pltpu.make_async_remote_copy(
            src_ref=src, dst_ref=dst, send_sem=ss, recv_sem=rs,
            device_id={"exp": peer}, device_id_type=MESH,
        )

    def loop(low, high, body):
        def step(i, c):
            body(i)
            return c
        lax.fori_loop(low, high, step, 0)

    barrier = pltpu.get_barrier_semaphore()
    loop(1, E, lambda d: pl.semaphore_signal(
        barrier, inc=1, device_id={"exp": lax.rem(ex + d, E)}, device_id_type=MESH))
    loop(1, S, lambda d: pl.semaphore_signal(
        barrier, inc=1, device_id={"seq": lax.rem(me + d, S)}, device_id_type=MESH))

    total_k = jnp.sum(k_ref[...].astype(F32), axis=1)
    total_v = jnp.sum(v_ref[...].astype(F32), axis=1)
    pool_send[...] = (jnp.concatenate([total_k, total_v], axis=0) * GROUP ** (-0.5)).astype(BF16)
    x_all[ex] = x_ref[...]
    kv_all[me] = jnp.zeros(kv_all.shape[1:], BF16)
    pl.semaphore_wait(barrier, S - 1 + E - 1)

    def send_x(d):
        peer = lax.rem(ex + d, E)
        exp_copy(x_ref, x_all.at[ex], x_ss.at[peer], x_rs.at[ex], peer).start()
    loop(1, E, send_x)

    def send_kv(peer):
        want = jnp.int32(0)
        for r in range(nb):
            for j in range(TOPK):
                t = chosen_ref[peer * nb + r, j] - me * nb
                want = jnp.where((t >= 0) & (t < nb), t, want)
        kv_send[peer, 0] = k_ref[want]
        kv_send[peer, 1] = v_ref[want]
        seq_copy(pool_send, pool_all.at[me], pool_ss.at[peer], pool_rs.at[me], peer).start()
        seq_copy(kv_send.at[peer], kv_all.at[me], kv_ss.at[peer], kv_rs.at[me], peer).start()

    def send_later(i):
        peer = S - 1 - i

        @pl.when(peer > me)
        def _():
            send_kv(peer)
    loop(0, S - 1, send_later)

    def near(tile):
        q0 = tile * TILE
        width = q0 + TILE
        causal = (
            lax.broadcasted_iota(jnp.int32, (TILE, width), 0) + q0
            >= lax.broadcasted_iota(jnp.int32, (TILE, width), 1)
        )
        for h in range(heads):
            cols = slice(h * HEAD, (h + 1) * HEAD)
            s = across(
                q_ref[q0:width, cols], k_ref[0:width // GROUP, :, cols].reshape(width, HEAD)) * scale
            s = jnp.where(causal, s, NEGATIVE)
            m = jnp.max(s, axis=1, keepdims=True)
            p = jnp.exp(s - m)
            l = jnp.sum(p, axis=1, keepdims=True)
            acc[q0:width, cols] = jnp.dot(
                p.astype(BF16), v_ref[0:width // GROUP, :, cols].reshape(width, HEAD), preferred_element_type=F32)
            top[h, q0:width] = jnp.broadcast_to(m, (TILE, HEAD))
            den[h, q0:width] = jnp.broadcast_to(l, (TILE, HEAD))

    def far(b):
        r0 = pl.multiple_of(b * GROUP, GROUP)
        npool = S * nb
        width = npool + TOPK * GROUP
        col = lax.broadcasted_iota(jnp.int32, (GROUP, width), 1)
        ok = col < me * nb
        sel_k, sel_v = [], []
        for j in range(TOPK):
            c = chosen_ref[me * nb + b, j]
            low = npool + j * GROUP
            limit = jnp.where(c >= 0, low + GROUP, low)
            ok = ok | ((col >= low) & (col < limit))
            src = lax.div(jnp.maximum(c, 0), nb)
            pair = kv_all[src]
            sel_k.append(pair[0])
            sel_v.append(pair[1])
        kk = jnp.concatenate([pool_k[...]] + sel_k, axis=0)
        vv = jnp.concatenate([pool_v[...]] + sel_v, axis=0)
        for h in range(heads):
            cols = slice(h * HEAD, (h + 1) * HEAD)
            s = across(q_ref[pl.ds(r0, GROUP), cols], kk[:, cols]) * scale
            s = jnp.where(ok, s, NEGATIVE)
            m0 = top[h, pl.ds(r0, GROUP)][:, 0:1]
            l0 = den[h, pl.ds(r0, GROUP)][:, 0:1]
            m = jnp.maximum(m0, jnp.max(s, axis=1, keepdims=True))
            p = jnp.exp(s - m)
            a = jnp.exp(m0 - m)
            l = l0 * a + jnp.sum(p, axis=1, keepdims=True)
            mixed = acc[pl.ds(r0, GROUP), cols] * a + jnp.dot(
                p.astype(BF16), vv[:, cols], preferred_element_type=F32)
            mixed = mixed / l
            mean = jnp.mean(mixed * mixed, axis=1, keepdims=True)
            attn_ref[pl.ds(r0, GROUP), cols] = (
                mixed * lax.rsqrt(mean + EPSILON) * gain_ref[0:1, cols]).astype(BF16)

    tiles = L // TILE
    early = tiles - 1
    for tile in range(early):
        near(tile)

    def wait_x(d):
        src = lax.rem(ex + d, E)
        exp_copy(x_ref, x_all.at[src], x_ss.at[src], x_rs.at[src], src).wait_recv()
    loop(1, E, wait_x)
    weight_copies[0].wait()
    weight_copies[1].wait()
    x = x_all[...].reshape(rows, Dl)
    chunk = 512

    def gate_up(n):
        c0 = pl.multiple_of(n * chunk, chunk)
        g = jnp.dot(x, wg[:, pl.ds(c0, chunk)], preferred_element_type=F32)
        u = jnp.dot(x, wu[:, pl.ds(c0, chunk)], preferred_element_type=F32)
        both = jnp.concatenate([g.reshape(S, own, chunk), u.reshape(S, own, chunk)], axis=1)
        part[:, :, pl.ds(c0, chunk)] = both.astype(BF16)
    loop(0, FF // chunk, gate_up)

    def send_rs(d):
        peer = lax.rem(me + d, S)
        seq_copy(part.at[peer], rs_all.at[me], rs_ss.at[peer], rs_rs.at[me], peer).start()
    loop(1, S, send_rs)

    for tile in range(early, tiles):
        near(tile)

    def wait_rs(d, total):
        src = lax.rem(me + d, S)
        seq_copy(part.at[src], rs_all.at[src], rs_ss.at[src], rs_rs.at[src], src).wait_recv()
        return total + rs_all[src].astype(F32)
    total = lax.fori_loop(1, S, wait_rs, part[me].astype(F32))
    g, u = total[:own], total[own:]
    hidden = (g / (1.0 + jnp.exp(-g)) * u).astype(BF16)
    hid_send[...] = hidden
    hid_all[me] = hidden

    def send_hid(d):
        peer = lax.rem(me + d, S)
        seq_copy(hid_send, hid_all.at[me], hid_ss.at[peer], hid_rs.at[me], peer).start()
    loop(1, S, send_hid)

    def wait_kv(src):
        @pl.when(src < me)
        def _():
            seq_copy(pool_send, pool_all.at[src], pool_ss.at[src], pool_rs.at[src], src).wait_recv()
            seq_copy(kv_send.at[src], kv_all.at[src], kv_ss.at[src], kv_rs.at[src], src).wait_recv()
    loop(0, S - 1, wait_kv)
    pools = pool_all[...].astype(F32)
    known = lax.broadcasted_iota(jnp.int32, pools.shape, 0) < me
    pools = jnp.where(known, pools, 0.0)
    pool_k[...] = pools[:, :nb].reshape(S * nb, C).astype(BF16)
    pool_v[...] = pools[:, nb:].reshape(S * nb, C).astype(BF16)
    half = nb // 2
    loop(0, half, far)

    def wait_hid(d):
        src = lax.rem(me + d, S)
        seq_copy(hid_send, hid_all.at[src], hid_ss.at[src], hid_rs.at[src], src).wait_recv()
    loop(1, S, wait_hid)
    weight_copies[2].wait()
    hid = hid_all[...].astype(F32).reshape(rows, FF).astype(BF16)
    out = jnp.dot(hid, wd[...], preferred_element_type=F32).astype(BF16).reshape(E, T, Dl)
    ret_send[...] = out
    ret_all[ex] = ret_send[ex]

    def send_ret(d):
        peer = lax.rem(ex + d, E)
        exp_copy(ret_send.at[peer], ret_all.at[ex], ret_ss.at[peer], ret_rs.at[ex], peer).start()
    loop(1, E, send_ret)
    loop(half, nb, far)

    def wait_ret(d):
        src = lax.rem(ex + d, E)
        exp_copy(ret_send.at[src], ret_all.at[src], ret_ss.at[src], ret_rs.at[src], src).wait_recv()
    loop(1, E, wait_ret)
    ids = ids_ref[...]
    rw = rw_ref[...]
    moe = jnp.zeros((T, Dl), F32)
    for e in range(E):
        coefficient = jnp.sum(jnp.where(ids == e, rw, 0.0), axis=1, keepdims=True)
        moe = moe + coefficient * ret_all[e].astype(F32)
    moe_ref[...] = moe.astype(BF16)

    def finish_exp(d):
        peer = lax.rem(ex + d, E)
        exp_copy(x_ref, x_all.at[ex], x_ss.at[peer], x_rs.at[ex], peer).wait_send()
        exp_copy(ret_send.at[peer], ret_all.at[ex], ret_ss.at[peer], ret_rs.at[ex], peer).wait_send()
    loop(1, E, finish_exp)

    def finish_seq(d):
        peer = lax.rem(me + d, S)
        seq_copy(part.at[peer], rs_all.at[me], rs_ss.at[peer], rs_rs.at[me], peer).wait_send()
        seq_copy(hid_send, hid_all.at[me], hid_ss.at[peer], hid_rs.at[me], peer).wait_send()

        @pl.when(peer > me)
        def _():
            seq_copy(pool_send, pool_all.at[me], pool_ss.at[peer], pool_rs.at[me], peer).wait_send()
            seq_copy(kv_send.at[peer], kv_all.at[me], kv_ss.at[peer], kv_rs.at[me], peer).wait_send()
    loop(1, S, finish_seq)


def local(S, E, queries, keys, values, head_gain, chosen, moe_input, expert_ids, route_weight, w_gate, w_up, w_down):
    L, C = queries.shape
    heads = C // HEAD
    nb = L // GROUP
    T, Dl = moe_input.shape
    FF = w_gate.shape[2]
    own = E * T // S
    vmem = pl.BlockSpec(memory_space=pltpu.VMEM)
    smem = pl.BlockSpec(memory_space=pltpu.SMEM)
    hbm = pl.BlockSpec(memory_space=pl.ANY)
    dma = pltpu.SemaphoreType.DMA
    return pl.pallas_call(
        functools.partial(kernel, S, E),
        out_shape=(
            jax.ShapeDtypeStruct((L, C), BF16),
            jax.ShapeDtypeStruct((T, Dl), BF16),
        ),
        in_specs=[vmem, vmem, vmem, vmem, smem, vmem, vmem, vmem, hbm, hbm, hbm],
        out_specs=(vmem, vmem),
        scratch_shapes=[
            pltpu.VMEM((Dl, FF), BF16),
            pltpu.VMEM((Dl, FF), BF16),
            pltpu.VMEM((FF, Dl), BF16),
            pltpu.VMEM((S, 2, GROUP, C), BF16),
            pltpu.VMEM((S, 2, GROUP, C), BF16),
            pltpu.VMEM((2 * nb, C), BF16),
            pltpu.VMEM((S, 2 * nb, C), BF16),
            pltpu.VMEM((S * nb, C), BF16),
            pltpu.VMEM((S * nb, C), BF16),
            pltpu.VMEM((L, C), F32),
            pltpu.VMEM((heads, L, HEAD), F32),
            pltpu.VMEM((heads, L, HEAD), F32),
            pltpu.VMEM((E, T, Dl), BF16),
            pltpu.VMEM((S, 2 * own, FF), BF16),
            pltpu.VMEM((S, 2 * own, FF), BF16),
            pltpu.VMEM((own, FF), BF16),
            pltpu.VMEM((S, own, FF), BF16),
            pltpu.VMEM((E, T, Dl), BF16),
            pltpu.VMEM((E, T, Dl), BF16),
            dma((3,)),
            dma((S,)), dma((S,)), dma((S,)), dma((S,)),
            dma((E,)), dma((E,)),
            dma((S,)), dma((S,)), dma((S,)), dma((S,)),
            dma((E,)), dma((E,)),
        ],
        compiler_params=pltpu.CompilerParams(
            collective_id=0, has_side_effects=True, vmem_limit_bytes=56 * 1024 * 1024
        ),
    )(
        queries, keys.reshape(nb, GROUP, C), values.reshape(nb, GROUP, C), head_gain.reshape(1, C), chosen, moe_input,
        expert_ids, route_weight, w_gate[0], w_up[0], w_down[0],
    )


def solution(mesh):
    placed = (
        P("seq", "exp"),
        P("seq", "exp"),
        P("seq", "exp"),
        P("exp"),
        P(),
        P("exp", "seq"),
        P("exp", None),
        P("exp", None),
        P("exp", "seq", None),
        P("exp", "seq", None),
        P("exp", None, "seq"),
    )
    return jax.shard_map(
        functools.partial(local, mesh.shape["seq"], mesh.shape["exp"]),
        mesh=mesh,
        in_specs=placed,
        out_specs=(P("seq", "exp"), P("exp", "seq")),
        check_vma=False,
    )
```

time: 156 us -> 50 us (0.32)
  the two profiles are of different devices: /device:TPU:0 before, /device:TPU:5 now
where the time goes in v1:
time: 50 us; the launch traced here: 49.7 us
  Pallas kernels  41.7 us (83%)
  local copies, waits for them, and re-layouts  7.31 us (15%)
  between operations  0.64 us (1%)
    pallas_call x1, Pallas kernels, local(): pl.pallas_call(functools.partial(kernel, S, E), out_shape=(jax.ShapeDtype...  41.7 us
    unnamed x5, local copies, waits for them, and re-layouts  7.31 us

profile of v1, /device:TPU:5, one launch (start us, length us, event | category | flops | bytes accessed | tf_op | source)
XLA Modules:
  0.0 49.7 jit_solution(993258905299771129)
XLA Ops:
  0.6 1.4 %copy.14.ids_ref = s32[16,2]{1,0:T(8,128)} copy(s32[16,2]{0,1:T(2,128)} %param.17) | data formatting | bytes 256 | tf_op args[6]
  2.0 1.3 %copy.15.rw_ref = f32[16,2]{1,0:T(8,128)} copy(f32[16,2]{0,1:T(2,128)} %param.18) | data formatting | bytes 256 | tf_op args[7]
  3.3 1.4 %copy.13.chosen_ref = s32[64,3]{1,0:T(8,128)} copy(s32[64,3]{0,1:T(4,128)} %param.15) | data formatting | bytes 1536 | tf_op args[4]
  4.7 41.7 %shard_map.122 = (bf16[512,512]{1,0:T(8,128)(2,1)}, bf16[16,896]{1,0:T(8,128)(2,1)}) custom-call(bf16[512,512]{1,0:T(8,128)(2,1)} %q_ref.1, bf16[8,64,512]{2,1,0:T(8,128)(2,1)} %bitcast.9, bf16[8,64,512]{2,1,0:T(8,128)(2,1)} %bitcast.10, f32[1,512]{1,0:T(1,128)} %bitcast.11, s32[64,3]{1,0:T(8,128)} %copy.13.chosen_ref, bf16[16,896]{1,0:T(8,128)(2,1)} %x_ref.1, ...), custom_call_target="tpu_custom_call" | custom-call | tf_op jit(solution)/shard_map/pallas_call | solution.py:277
  46.4 1.9 %copy.18 = bf16[512,512]{1,0:T(8,128)(2,1)} copy(bf16[512,512]{1,0:T(8,128)(2,1)} %get-tuple-element.4) | data formatting | bytes 1048576
  48.3 1.4 %copy.19 = bf16[16,896]{1,0:T(8,128)(2,1)} copy(bf16[16,896]{1,0:T(8,128)(2,1)} %get-tuple-element.5) | data formatting | bytes 57344

commit v2 on v1

--- a/solution.py
+++ b/solution.py
@@ -11,6 +11,7 @@
 GROUP = 64
 TOPK = 3
 TILE = 128
+CHUNK = 512
 EPSILON = 1e-06
 NEGATIVE = -1e30
 MESH = pl.DeviceIdType.MESH
@@ -24,15 +25,16 @@
 
 def kernel(
     S, E,
-    q_ref, k_ref, v_ref, gain_ref, chosen_ref, x_ref, ids_ref, rw_ref, wg_hbm, wu_hbm, wd_hbm,
+    q_hbm, k_hbm, v_hbm, gain_ref, chosen_ref, x_ref, ids_ref, rw_ref, wg_hbm, wu_hbm, wd_hbm,
     attn_ref, moe_ref,
-    wg, wu, wd, kv_send, kv_all, pool_send, pool_all, pool_k, pool_v,
-    acc, top, den, x_all, part, rs_all, hid_send, hid_all, ret_send, ret_all,
-    w_sem, kv_ss, kv_rs, pool_ss, pool_rs, x_ss, x_rs, rs_ss, rs_rs, hid_ss, hid_rs, ret_ss, ret_rs,
+    q_ref, k_ref, v_ref, wg, wu, wd, k_send, k_all, v_send, v_all, pool_send, pool_all, pool_k, pool_v,
+    acc, top, den, x_all, kept, pair_send, pair_all, rs_send, rs_all, hid_send, hid_all, ret_send, ret_all,
+    w_sem, k_ss, k_rs, v_ss, v_rs, pool_ss, pool_rs, x_ss, x_rs, pair_ss, pair_rs, rs_ss, rs_rs,
+    hid_ss, hid_rs, ret_ss, ret_rs,
 ):
     me = lax.axis_index("seq")
     ex = lax.axis_index("exp")
-    L, C = q_ref.shape
+    L, C = q_hbm.shape
     heads = C // HEAD
     nb = L // GROUP
     T, Dl = x_ref.shape
@@ -43,10 +45,13 @@
 
     weight_copies = [
         pltpu.make_async_copy(src, dst, w_sem.at[i])
-        for i, (src, dst) in enumerate(((wg_hbm, wg), (wu_hbm, wu), (wd_hbm, wd)))
+        for i, (src, dst) in enumerate((
+            (wg_hbm, wg), (wu_hbm, wu), (wd_hbm, wd),
+            (k_hbm, k_ref), (v_hbm, v_ref), (q_hbm, q_ref),
+        ))
     ]
-    for copy in weight_copies:
-        copy.start()
+    for i in (3, 4, 5, 0, 1, 2):
+        weight_copies[i].start()
 
     def seq_copy(src, dst, ss, rs, peer):
         return pltpu.make_async_remote_copy(
@@ -72,11 +77,7 @@
     loop(1, S, lambda d: pl.semaphore_signal(
         barrier, inc=1, device_id={"seq": lax.rem(me + d, S)}, device_id_type=MESH))
 
-    total_k = jnp.sum(k_ref[...].astype(F32), axis=1)
-    total_v = jnp.sum(v_ref[...].astype(F32), axis=1)
-    pool_send[...] = (jnp.concatenate([total_k, total_v], axis=0) * GROUP ** (-0.5)).astype(BF16)
     x_all[ex] = x_ref[...]
-    kv_all[me] = jnp.zeros(kv_all.shape[1:], BF16)
     pl.semaphore_wait(barrier, S - 1 + E - 1)
 
     def send_x(d):
@@ -84,16 +85,24 @@
         exp_copy(x_ref, x_all.at[ex], x_ss.at[peer], x_rs.at[ex], peer).start()
     loop(1, E, send_x)
 
+    weight_copies[3].wait()
+    weight_copies[4].wait()
+    total_k = jnp.sum(k_ref[...].astype(F32), axis=1)
+    total_v = jnp.sum(v_ref[...].astype(F32), axis=1)
+    pool_send[...] = (jnp.concatenate([total_k, total_v], axis=0) * GROUP ** (-0.5)).astype(BF16)
+    k_all[me] = jnp.zeros(k_all.shape[1:], BF16)
+    v_all[me] = jnp.zeros(v_all.shape[1:], BF16)
+
     def send_kv(peer):
         want = jnp.int32(0)
         for r in range(nb):
             for j in range(TOPK):
-                t = chosen_ref[peer * nb + r, j] - me * nb
+                t = chosen_ref[j, peer * nb + r] - me * nb
                 want = jnp.where((t >= 0) & (t < nb), t, want)
-        kv_send[peer, 0] = k_ref[want]
-        kv_send[peer, 1] = v_ref[want]
+        k_send[peer] = k_ref[want]
+        v_send[peer] = v_ref[want]
         seq_copy(pool_send, pool_all.at[me], pool_ss.at[peer], pool_rs.at[me], peer).start()
-        seq_copy(kv_send.at[peer], kv_all.at[me], kv_ss.at[peer], kv_rs.at[me], peer).start()
+        seq_copy(k_send.at[peer], k_all.at[me], k_ss.at[peer], k_rs.at[me], peer).start()
 
     def send_later(i):
         peer = S - 1 - i
@@ -102,6 +111,15 @@
         def _():
             send_kv(peer)
     loop(0, S - 1, send_later)
+
+    def send_values(i):
+        peer = S - 1 - i
+
+        @pl.when(peer > me)
+        def _():
+            seq_copy(v_send.at[peer], v_all.at[me], v_ss.at[peer], v_rs.at[me], peer).start()
+    loop(0, S - 1, send_values)
+    weight_copies[5].wait()
 
     def near(tile):
         q0 = tile * TILE
@@ -131,14 +149,13 @@
         ok = col < me * nb
         sel_k, sel_v = [], []
         for j in range(TOPK):
-            c = chosen_ref[me * nb + b, j]
+            c = chosen_ref[j, me * nb + b]
             low = npool + j * GROUP
             limit = jnp.where(c >= 0, low + GROUP, low)
             ok = ok | ((col >= low) & (col < limit))
             src = lax.div(jnp.maximum(c, 0), nb)
-            pair = kv_all[src]
-            sel_k.append(pair[0])
-            sel_v.append(pair[1])
+            sel_k.append(k_all[src])
+            sel_v.append(v_all[src])
         kk = jnp.concatenate([pool_k[...]] + sel_k, axis=0)
         vv = jnp.concatenate([pool_v[...]] + sel_v, axis=0)
         for h in range(heads):
@@ -170,33 +187,63 @@
     weight_copies[0].wait()
     weight_copies[1].wait()
     x = x_all[...].reshape(rows, Dl)
-    chunk = 512
+    chunk = CHUNK
+
+    chunks = FF // chunk
+    pairs = S // 2
+    side = lax.rem(me, 2)
+    spot = lax.div(me, 2)
+    partner = me + 1 - 2 * side
+
+    def pair_copy(n):
+        return seq_copy(pair_send.at[n], pair_all.at[n], pair_ss.at[n], pair_rs.at[n], partner)
 
     def gate_up(n):
         c0 = pl.multiple_of(n * chunk, chunk)
         g = jnp.dot(x, wg[:, pl.ds(c0, chunk)], preferred_element_type=F32)
         u = jnp.dot(x, wu[:, pl.ds(c0, chunk)], preferred_element_type=F32)
         both = jnp.concatenate([g.reshape(S, own, chunk), u.reshape(S, own, chunk)], axis=1)
-        part[:, :, pl.ds(c0, chunk)] = both.astype(BF16)
-    loop(0, FF // chunk, gate_up)
-
-    def send_rs(d):
-        peer = lax.rem(me + d, S)
-        seq_copy(part.at[peer], rs_all.at[me], rs_ss.at[peer], rs_rs.at[me], peer).start()
-    loop(1, S, send_rs)
+        both = both.reshape(pairs, 2, 2 * own, chunk)
+        kept[n] = jnp.where(side == 0, both[:, 0], both[:, 1])
+        pair_send[n] = jnp.where(side == 0, both[:, 1], both[:, 0])
+        pair_copy(n).start()
+    loop(0, chunks, gate_up)
+
+    def rs_copy(n, d, sender, receiver):
+        return seq_copy(
+            rs_send.at[n, receiver], rs_all.at[n, sender],
+            rs_ss.at[n, receiver], rs_rs.at[n, sender], 2 * receiver + side)
+
+    def send_rs(n):
+        pair_copy(n).wait_recv()
+        both = kept[n] + pair_all[n]
+        kept[n] = both
+        rs_send[n] = both.astype(BF16)
+
+        def each(d):
+            rs_copy(n, d, spot, lax.rem(spot + d, pairs)).start()
+        loop(1, pairs, each)
+    loop(0, chunks, send_rs)
 
     for tile in range(early, tiles):
         near(tile)
 
-    def wait_rs(d, total):
-        src = lax.rem(me + d, S)
-        seq_copy(part.at[src], rs_all.at[src], rs_ss.at[src], rs_rs.at[src], src).wait_recv()
-        return total + rs_all[src].astype(F32)
-    total = lax.fori_loop(1, S, wait_rs, part[me].astype(F32))
-    g, u = total[:own], total[own:]
-    hidden = (g / (1.0 + jnp.exp(-g)) * u).astype(BF16)
-    hid_send[...] = hidden
-    hid_all[me] = hidden
+    def wait_rs(n):
+        total = kept[n, spot]
+
+        def each(d, total):
+            src = lax.rem(spot + d, pairs)
+            seq_copy(
+                rs_send.at[n, src], rs_all.at[n, src], rs_ss.at[n, src], rs_rs.at[n, src],
+                2 * src + side).wait_recv()
+            return total + rs_all[n, src].astype(F32)
+        total = lax.fori_loop(1, pairs, each, total)
+        g, u = total[:own], total[own:]
+        hidden = (g / (1.0 + jnp.exp(-g)) * u).astype(BF16)
+        c0 = pl.multiple_of(n * chunk, chunk)
+        hid_send[:, pl.ds(c0, chunk)] = hidden
+    loop(0, chunks, wait_rs)
+    hid_all[me] = hid_send[...]
 
     def send_hid(d):
         peer = lax.rem(me + d, S)
@@ -207,7 +254,8 @@
         @pl.when(src < me)
         def _():
             seq_copy(pool_send, pool_all.at[src], pool_ss.at[src], pool_rs.at[src], src).wait_recv()
-            seq_copy(kv_send.at[src], kv_all.at[src], kv_ss.at[src], kv_rs.at[src], src).wait_recv()
+            seq_copy(k_send.at[src], k_all.at[src], k_ss.at[src], k_rs.at[src], src).wait_recv()
+            seq_copy(v_send.at[src], v_all.at[src], v_ss.at[src], v_rs.at[src], src).wait_recv()
     loop(0, S - 1, wait_kv)
     pools = pool_all[...].astype(F32)
     known = lax.broadcasted_iota(jnp.int32, pools.shape, 0) < me
@@ -233,16 +281,24 @@
     loop(1, E, send_ret)
     loop(half, nb, far)
 
+    ids = ids_ref[...]
+    rw = rw_ref[...]
+    diagonal = (
+        lax.broadcasted_iota(jnp.int32, (T, T), 0) == lax.broadcasted_iota(jnp.int32, (T, T), 1)
+    )
+    coefficients = []
+    for e in range(E):
+        row = jnp.sum(jnp.where(ids == e, rw, 0.0), axis=0, keepdims=True)
+        square = jnp.where(diagonal, jnp.broadcast_to(row, (T, T)), 0.0)
+        coefficients.append(jnp.sum(square, axis=1, keepdims=True))
+
     def wait_ret(d):
         src = lax.rem(ex + d, E)
         exp_copy(ret_send.at[src], ret_all.at[src], ret_ss.at[src], ret_rs.at[src], src).wait_recv()
     loop(1, E, wait_ret)
-    ids = ids_ref[...]
-    rw = rw_ref[...]
     moe = jnp.zeros((T, Dl), F32)
     for e in range(E):
-        coefficient = jnp.sum(jnp.where(ids == e, rw, 0.0), axis=1, keepdims=True)
-        moe = moe + coefficient * ret_all[e].astype(F32)
+        moe = moe + coefficients[e] * ret_all[e].astype(F32)
     moe_ref[...] = moe.astype(BF16)
 
     def finish_exp(d):
@@ -253,14 +309,19 @@
 
     def finish_seq(d):
         peer = lax.rem(me + d, S)
-        seq_copy(part.at[peer], rs_all.at[me], rs_ss.at[peer], rs_rs.at[me], peer).wait_send()
         seq_copy(hid_send, hid_all.at[me], hid_ss.at[peer], hid_rs.at[me], peer).wait_send()
 
         @pl.when(peer > me)
         def _():
             seq_copy(pool_send, pool_all.at[me], pool_ss.at[peer], pool_rs.at[me], peer).wait_send()
-            seq_copy(kv_send.at[peer], kv_all.at[me], kv_ss.at[peer], kv_rs.at[me], peer).wait_send()
+            seq_copy(k_send.at[peer], k_all.at[me], k_ss.at[peer], k_rs.at[me], peer).wait_send()
+            seq_copy(v_send.at[peer], v_all.at[me], v_ss.at[peer], v_rs.at[me], peer).wait_send()
     loop(1, S, finish_seq)
+
+    def finish_rs(n):
+        pair_copy(n).wait_send()
+        loop(1, pairs, lambda d: rs_copy(n, d, spot, lax.rem(spot + d, pairs)).wait_send())
+    loop(0, chunks, finish_rs)
 
 
 def local(S, E, queries, keys, values, head_gain, chosen, moe_input, expert_ids, route_weight, w_gate, w_up, w_down):
@@ -270,6 +331,7 @@
     T, Dl = moe_input.shape
     FF = w_gate.shape[2]
     own = E * T // S
+    chunks = FF // CHUNK
     vmem = pl.BlockSpec(memory_space=pltpu.VMEM)
     smem = pl.BlockSpec(memory_space=pltpu.SMEM)
     hbm = pl.BlockSpec(memory_space=pl.ANY)
@@ -280,14 +342,19 @@
             jax.ShapeDtypeStruct((L, C), BF16),
             jax.ShapeDtypeStruct((T, Dl), BF16),
         ),
-        in_specs=[vmem, vmem, vmem, vmem, smem, vmem, vmem, vmem, hbm, hbm, hbm],
+        in_specs=[hbm, hbm, hbm, vmem, smem, vmem, vmem, vmem, hbm, hbm, hbm],
         out_specs=(vmem, vmem),
         scratch_shapes=[
+            pltpu.VMEM((L, C), BF16),
+            pltpu.VMEM((nb, GROUP, C), BF16),
+            pltpu.VMEM((nb, GROUP, C), BF16),
             pltpu.VMEM((Dl, FF), BF16),
             pltpu.VMEM((Dl, FF), BF16),
             pltpu.VMEM((FF, Dl), BF16),
-            pltpu.VMEM((S, 2, GROUP, C), BF16),
-            pltpu.VMEM((S, 2, GROUP, C), BF16),
+            pltpu.VMEM((S, GROUP, C), BF16),
+            pltpu.VMEM((S, GROUP, C), BF16),
+            pltpu.VMEM((S, GROUP, C), BF16),
+            pltpu.VMEM((S, GROUP, C), BF16),
             pltpu.VMEM((2 * nb, C), BF16),
             pltpu.VMEM((S, 2 * nb, C), BF16),
             pltpu.VMEM((S * nb, C), BF16),
@@ -296,24 +363,28 @@
             pltpu.VMEM((heads, L, HEAD), F32),
             pltpu.VMEM((heads, L, HEAD), F32),
             pltpu.VMEM((E, T, Dl), BF16),
-            pltpu.VMEM((S, 2 * own, FF), BF16),
-            pltpu.VMEM((S, 2 * own, FF), BF16),
+            pltpu.VMEM((chunks, S // 2, 2 * own, CHUNK), F32),
+            pltpu.VMEM((chunks, S // 2, 2 * own, CHUNK), F32),
+            pltpu.VMEM((chunks, S // 2, 2 * own, CHUNK), F32),
+            pltpu.VMEM((chunks, S // 2, 2 * own, CHUNK), BF16),
+            pltpu.VMEM((chunks, S // 2, 2 * own, CHUNK), BF16),
             pltpu.VMEM((own, FF), BF16),
             pltpu.VMEM((S, own, FF), BF16),
             pltpu.VMEM((E, T, Dl), BF16),
             pltpu.VMEM((E, T, Dl), BF16),
-            dma((3,)),
-            dma((S,)), dma((S,)), dma((S,)), dma((S,)),
+            dma((6,)),
+            dma((S,)), dma((S,)), dma((S,)), dma((S,)), dma((S,)), dma((S,)),
             dma((E,)), dma((E,)),
-            dma((S,)), dma((S,)), dma((S,)), dma((S,)),
+            dma((chunks,)), dma((chunks,)), dma((chunks, S // 2)), dma((chunks, S // 2)),
+            dma((S,)), dma((S,)),
             dma((E,)), dma((E,)),
         ],
         compiler_params=pltpu.CompilerParams(
             collective_id=0, has_side_effects=True, vmem_limit_bytes=56 * 1024 * 1024
         ),
     )(
-        queries, keys.reshape(nb, GROUP, C), values.reshape(nb, GROUP, C), head_gain.reshape(1, C), chosen, moe_input,
-        expert_ids, route_weight, w_gate[0], w_up[0], w_down[0],
+        queries, keys.reshape(nb, GROUP, C), values.reshape(nb, GROUP, C), head_gain.reshape(1, C), chosen.T, moe_input,
+        expert_ids.T, route_weight.T, w_gate[0], w_up[0], w_down[0],
     )
 
 

time: 50 us -> 42.1 us (0.84)
  the two profiles are of different devices: /device:TPU:5 before, /device:TPU:6 now
where the time goes in v2:
time: 42.1 us; the launch traced here: 41.8 us
  Pallas kernels  38 us (90%)
  local copies, waits for them, and re-layouts  3.23 us (8%)
  between operations  0.64 us (2%)
    pallas_call x1, Pallas kernels, local(): pl.pallas_call(functools.partial(kernel, S, E), out_shape=(jax.ShapeDtype...  38 us
    unnamed x2, local copies, waits for them, and re-layouts  3.23 us

profile of v2, /device:TPU:6, one launch (start us, length us, event | category | flops | bytes accessed | tf_op | source)
XLA Modules:
  0.0 41.8 jit_solution(17534739042206479756)
XLA Ops:
  0.6 38.0 %shard_map.122 = (bf16[512,512]{1,0:T(8,128)(2,1)}, bf16[16,896]{1,0:T(8,128)(2,1)}) custom-call(bf16[512,512]{1,0:T(8,128)(2,1)} %q_hbm.1, bf16[8,64,512]{2,1,0:T(8,128)(2,1)} %bitcast.12, bf16[8,64,512]{2,1,0:T(8,128)(2,1)} %bitcast.13, f32[1,512]{1,0:T(1,128)} %bitcast.14, s32[3,64]{1,0:T(4,128)} %bitcast.15, bf16[16,896]{1,0:T(8,128)(2,1)} %x_ref.1, ...), custom_call_target="tpu_custom_call" | custom-call | tf_op jit(solution)/shard_map/pallas_call | solution.py:339
  38.6 1.9 %copy.15 = bf16[512,512]{1,0:T(8,128)(2,1)} copy(bf16[512,512]{1,0:T(8,128)(2,1)} %get-tuple-element.4) | data formatting | bytes 1048576
  40.5 1.4 %copy.16 = bf16[16,896]{1,0:T(8,128)(2,1)} copy(bf16[16,896]{1,0:T(8,128)(2,1)} %get-tuple-element.5) | data formatting | bytes 57344

commit v3 on v2

--- a/solution.py
+++ b/solution.py
@@ -9,6 +9,7 @@
 
 HEAD = 128
 GROUP = 64
+FAR = 2
 TOPK = 3
 TILE = 128
 CHUNK = 512
@@ -118,7 +119,6 @@
         @pl.when(peer > me)
         def _():
             seq_copy(v_send.at[peer], v_all.at[me], v_ss.at[peer], v_rs.at[me], peer).start()
-    loop(0, S - 1, send_values)
     weight_copies[5].wait()
 
     def near(tile):
@@ -141,36 +141,44 @@
             top[h, q0:width] = jnp.broadcast_to(m, (TILE, HEAD))
             den[h, q0:width] = jnp.broadcast_to(l, (TILE, HEAD))
 
-    def far(b):
-        r0 = pl.multiple_of(b * GROUP, GROUP)
+    def far(step):
         npool = S * nb
         width = npool + TOPK * GROUP
         col = lax.broadcasted_iota(jnp.int32, (GROUP, width), 1)
-        ok = col < me * nb
-        sel_k, sel_v = [], []
-        for j in range(TOPK):
-            c = chosen_ref[j, me * nb + b]
-            low = npool + j * GROUP
-            limit = jnp.where(c >= 0, low + GROUP, low)
-            ok = ok | ((col >= low) & (col < limit))
-            src = lax.div(jnp.maximum(c, 0), nb)
-            sel_k.append(k_all[src])
-            sel_v.append(v_all[src])
-        kk = jnp.concatenate([pool_k[...]] + sel_k, axis=0)
-        vv = jnp.concatenate([pool_v[...]] + sel_v, axis=0)
-        for h in range(heads):
-            cols = slice(h * HEAD, (h + 1) * HEAD)
-            s = across(q_ref[pl.ds(r0, GROUP), cols], kk[:, cols]) * scale
-            s = jnp.where(ok, s, NEGATIVE)
-            m0 = top[h, pl.ds(r0, GROUP)][:, 0:1]
-            l0 = den[h, pl.ds(r0, GROUP)][:, 0:1]
+        work = []
+        for i in range(FAR):
+            b = step * FAR + i
+            r0 = pl.multiple_of(b * GROUP, GROUP)
+            ok = col < me * nb
+            srcs = []
+            for j in range(TOPK):
+                c = chosen_ref[j, me * nb + b]
+                low = npool + j * GROUP
+                limit = jnp.where(c >= 0, low + GROUP, low)
+                ok = ok | ((col >= low) & (col < limit))
+                srcs.append(lax.div(jnp.maximum(c, 0), nb))
+            kk = jnp.concatenate([pool_k[...]] + [k_all[src] for src in srcs], axis=0)
+            vv = jnp.concatenate([pool_v[...]] + [v_all[src] for src in srcs], axis=0)
+            for h in range(heads):
+                cols = slice(h * HEAD, (h + 1) * HEAD)
+                s = across(q_ref[pl.ds(r0, GROUP), cols], kk[:, cols]) * scale
+                work.append((h, r0, cols, jnp.where(ok, s, NEGATIVE), vv[:, cols]))
+        tops = []
+        for h, r0, cols, s, vv in work:
+            m0 = top[h, pl.ds(r0, GROUP)]
             m = jnp.maximum(m0, jnp.max(s, axis=1, keepdims=True))
-            p = jnp.exp(s - m)
-            a = jnp.exp(m0 - m)
-            l = l0 * a + jnp.sum(p, axis=1, keepdims=True)
-            mixed = acc[pl.ds(r0, GROUP), cols] * a + jnp.dot(
-                p.astype(BF16), vv[:, cols], preferred_element_type=F32)
-            mixed = mixed / l
+            tops.append((m, jnp.exp(m0 - m)))
+        probs = []
+        for (h, r0, cols, s, vv), (m, a) in zip(work, tops):
+            wide = jnp.concatenate([m] * (-(-width // HEAD)), axis=1)[:, :width]
+            p = jnp.exp(s - wide)
+            l = den[h, pl.ds(r0, GROUP)] * a + jnp.sum(p, axis=1, keepdims=True)
+            probs.append((p.astype(BF16), l))
+        outs = []
+        for (h, r0, cols, s, vv), (m, a), (p, l) in zip(work, tops, probs):
+            mixed = acc[pl.ds(r0, GROUP), cols] * a + jnp.dot(p, vv, preferred_element_type=F32)
+            outs.append(mixed / l)
+        for (h, r0, cols, s, vv), mixed in zip(work, outs):
             mean = jnp.mean(mixed * mixed, axis=1, keepdims=True)
             attn_ref[pl.ds(r0, GROUP), cols] = (
                 mixed * lax.rsqrt(mean + EPSILON) * gain_ref[0:1, cols]).astype(BF16)
@@ -249,7 +257,24 @@
         peer = lax.rem(me + d, S)
         seq_copy(hid_send, hid_all.at[me], hid_ss.at[peer], hid_rs.at[me], peer).start()
     loop(1, S, send_hid)
-
+    loop(0, S - 1, send_values)
+
+    steps = nb // FAR
+
+    def wait_hid(d):
+        src = lax.rem(me + d, S)
+        seq_copy(hid_send, hid_all.at[src], hid_ss.at[src], hid_rs.at[src], src).wait_recv()
+    loop(1, S, wait_hid)
+    weight_copies[2].wait()
+    hid = hid_all[...].astype(F32).reshape(rows, FF).astype(BF16)
+    out = jnp.dot(hid, wd[...], preferred_element_type=F32).astype(BF16).reshape(E, T, Dl)
+    ret_send[...] = out
+    ret_all[ex] = ret_send[ex]
+
+    def send_ret(d):
+        peer = lax.rem(ex + d, E)
+        exp_copy(ret_send.at[peer], ret_all.at[ex], ret_ss.at[peer], ret_rs.at[ex], peer).start()
+    loop(1, E, send_ret)
     def wait_kv(src):
         @pl.when(src < me)
         def _():
@@ -262,24 +287,8 @@
     pools = jnp.where(known, pools, 0.0)
     pool_k[...] = pools[:, :nb].reshape(S * nb, C).astype(BF16)
     pool_v[...] = pools[:, nb:].reshape(S * nb, C).astype(BF16)
-    half = nb // 2
-    loop(0, half, far)
-
-    def wait_hid(d):
-        src = lax.rem(me + d, S)
-        seq_copy(hid_send, hid_all.at[src], hid_ss.at[src], hid_rs.at[src], src).wait_recv()
-    loop(1, S, wait_hid)
-    weight_copies[2].wait()
-    hid = hid_all[...].astype(F32).reshape(rows, FF).astype(BF16)
-    out = jnp.dot(hid, wd[...], preferred_element_type=F32).astype(BF16).reshape(E, T, Dl)
-    ret_send[...] = out
-    ret_all[ex] = ret_send[ex]
-
-    def send_ret(d):
-        peer = lax.rem(ex + d, E)
-        exp_copy(ret_send.at[peer], ret_all.at[ex], ret_ss.at[peer], ret_rs.at[ex], peer).start()
-    loop(1, E, send_ret)
-    loop(half, nb, far)
+    loop(0, steps, far)
+
 
     ids = ids_ref[...]
     rw = rw_ref[...]

time: 42.1 us -> 34.6 us (0.82)
  the two profiles are of different devices: /device:TPU:6 before, /device:TPU:0 now
where the time goes in v3:
time: 34.6 us; the launch traced here: 34.3 us
  Pallas kernels  30.4 us (88%)
  local copies, waits for them, and re-layouts  3.23 us (9%)
  between operations  0.64 us (2%)
    pallas_call x1, Pallas kernels, local(): pl.pallas_call(functools.partial(kernel, S, E), out_shape=(jax.ShapeDtype...  30.4 us
    unnamed x2, local copies, waits for them, and re-layouts  3.23 us

profile of v3, /device:TPU:0, one launch (start us, length us, event | category | flops | bytes accessed | tf_op | source)
XLA Modules:
  0.0 34.3 jit_solution(10056741204529740793)
XLA Ops:
  0.6 30.4 %shard_map.122 = (bf16[512,512]{1,0:T(8,128)(2,1)}, bf16[16,896]{1,0:T(8,128)(2,1)}) custom-call(bf16[512,512]{1,0:T(8,128)(2,1)} %q_hbm.1, bf16[8,64,512]{2,1,0:T(8,128)(2,1)} %bitcast.12, bf16[8,64,512]{2,1,0:T(8,128)(2,1)} %bitcast.13, f32[1,512]{1,0:T(1,128)} %bitcast.14, s32[3,64]{1,0:T(4,128)} %bitcast.15, bf16[16,896]{1,0:T(8,128)(2,1)} %x_ref.1, ...), custom_call_target="tpu_custom_call" | custom-call | tf_op jit(solution)/shard_map/pallas_call | solution.py:348
  31.1 1.9 %copy.15 = bf16[512,512]{1,0:T(8,128)(2,1)} copy(bf16[512,512]{1,0:T(8,128)(2,1)} %get-tuple-element.4) | data formatting | bytes 1048576
  32.9 1.4 %copy.16 = bf16[16,896]{1,0:T(8,128)(2,1)} copy(bf16[16,896]{1,0:T(8,128)(2,1)} %get-tuple-element.5) | data formatting | bytes 57344
